TPU v7x, 32 devices: a whole 2x2x4 slice. The times are simulated.
32 devices in a mesh: gx: 4 (over x, core), gy: 4 (over z), gz: 2 (over y).
Axes of the slice: x: 2, y: 2, z: 4, core: 2. Of those that a mesh axis runs over, the one named last changes fastest.
Arguments:
- displacement: float32 [3, 32, 32, 256], P(None, 'gx', 'gy', 'gz'), may hold values from -0.25 to 0.25
- bond_intact: int32 [61, 32, 32, 256], P(None, 'gx', 'gy', 'gz'), may hold values 0 or 1
Outputs:
- force: float32 [3, 32, 32, 256], P(None, 'gx', 'gy', 'gz')
- dilatation: float32 [32, 32, 256], P('gx', 'gy', 'gz')
All inputs are finite; a program needn't handle non-finite values. No bound on the sum of `bond_intact` on one device may be relied on, other than what follows from the above.
Results may differ from a plain program's by a relative error of at most 0.000063.
Values sent between devices are 32-bit elements; how exact they have to be, the bound alone decides.
A program may use at most 128 MiB of HBM per device.

v0:
```python
import math

import jax
import jax.numpy as jnp
from jax import lax
from jax.sharding import PartitionSpec as P

bulk_modulus = 150.0
shear_modulus = 25.0
soft_stretch = 0.05


def extended_2(x, sides, width):
    for axis, dim in sides:
        size, length = (lax.axis_size(axis), x.shape[dim])
        up = [(i, (i + 1) % size) for i in range(size - 1)]
        down = [(j, i) for i, j in up]
        last = lax.slice_in_dim(x, length - width, length, axis=dim)
        first = lax.slice_in_dim(x, 0, width, axis=dim)
        before = lax.ppermute(last, axis, up)
        after = lax.ppermute(first, axis, down)
        x = jnp.concatenate([before, x, after], axis=dim)
    return x


def passed_along(value, axis, steps):
    count = lax.axis_size(axis)
    first, last = (max(0, -steps), min(count, count - steps))
    return lax.ppermute(value, axis, [(source, source + steps) for source in range(first, last)])


def bond_offsets():
    chosen = []
    for step_x in range(0, 4):
        for step_y in range(-3, 4):
            for step_z in range(-3, 4):
                if step_x * step_x + step_y * step_y + step_z * step_z > 9:
                    continue
                if step_x > 0 or (step_x == 0 and (step_y > 0 or (step_y == 0 and step_z > 0))):
                    chosen.append((step_x, step_y, step_z))
    return chosen


def weighted_volume():
    total = 0.0
    for offset in bond_offsets():
        squared = offset[0] * offset[0] + offset[1] * offset[1] + offset[2] * offset[2]
        total = total + math.exp(-squared / 9.0) * squared
    return 2.0 * total


def offset_terms(offset):
    squared = offset[0] * offset[0] + offset[1] * offset[1] + offset[2] * offset[2]
    return (math.sqrt(squared), math.exp(-squared / 9.0))


def bond_vector(owner_u, partner_u, offset):
    pieces = [offset[number] + partner_u[number] - owner_u[number] for number in range(3)]
    length = jnp.sqrt(pieces[0] * pieces[0] + pieces[1] * pieces[1] + pieces[2] * pieces[2])
    return (pieces, length)


def dilatation_term(length, offset, intact, volume):
    radius, weight = offset_terms(offset)
    return intact * (3.0 / volume * weight * radius) * (length - radius)


def force_scalar(length, offset, theta_owner, theta_partner, intact, volume):
    radius, weight = offset_terms(offset)
    both = theta_owner + theta_partner
    extension = length - radius
    ratio = extension / (radius * soft_stretch)
    soften = 1.0 / (1.0 + ratio * ratio)
    total = (
        3.0 * bulk_modulus / volume * weight * radius * both
        + 15.0 * shear_modulus / volume * weight * (2.0 * extension - both * (radius / 3.0))
    )
    return intact * soften * total / length


def window(array, offset, extent):
    return array[
        ...,
        3 + offset[0] : 3 + offset[0] + extent[0],
        3 + offset[1] : 3 + offset[1] + extent[1],
        3 + offset[2] : 3 + offset[2] + extent[2],
    ]


def add_block(target, block, offset):
    starts = (0,) * (target.ndim - 3) + tuple((3 + shift_step for shift_step in offset))
    current = lax.dynamic_slice(target, starts, block.shape)
    return lax.dynamic_update_slice(target, current + block, starts)


def fold_back(extended, dimensions):
    for dimension in dimensions:
        length = extended.shape[dimension] - 12
        middle = lax.slice_in_dim(extended, 6, 6 + length, axis=dimension)
        bottom = lax.slice_in_dim(extended, 0, 3, axis=dimension)
        top_rim = lax.slice_in_dim(extended, length + 9, length + 12, axis=dimension)
        first = lax.slice_in_dim(middle, 0, 3, axis=dimension)
        middle = lax.dynamic_update_slice_in_dim(middle, first + bottom, 0, dimension)
        last = lax.slice_in_dim(middle, length - 3, length, axis=dimension)
        middle = lax.dynamic_update_slice_in_dim(middle, last + top_rim, length - 3, dimension)
        extended = middle
    return extended


def inside_line(position, count, total):
    coords = position * count - 3 + jnp.arange(count + 6, dtype=jnp.int32)
    return ((coords >= 0) & (coords < total)).astype(jnp.float32)


def upper_displacement(field):
    beside = extended_2(field, (("gy", 2), ("gz", 3)), 3)
    above = passed_along(beside[:, 0:3], "gx", -1)
    return jnp.concatenate([jnp.zeros_like(above), beside, above], axis=1)


def upper_dilatation(theta):
    beside = extended_2(theta, (("gy", 1), ("gz", 2)), 3)
    above = passed_along(beside[0:3], "gx", -1)
    return jnp.concatenate([jnp.zeros_like(above), beside, above], axis=0)


def upper_fold_parts(theta_sum):
    count = theta_sum.shape[0] - 6
    arrived = passed_along(theta_sum[count + 3 : count + 6], "gx", 1)
    inner = theta_sum[3 : count + 3]
    inner = lax.dynamic_update_slice_in_dim(inner, inner[0:3] + arrived, 0, 0)
    beside = extended_2(inner, (("gy", 1), ("gz", 2)), 3)
    return fold_back(beside, (1, 2))


def upper_fold_reactions(force_sum):
    count = force_sum.shape[1] - 6
    arrived = passed_along(force_sum[:, count + 3 : count + 6], "gx", 1)
    inner = force_sum[:, 3 : count + 3]
    inner = lax.dynamic_update_slice_in_dim(inner, inner[:, 0:3] + arrived, 0, 1)
    beside = extended_2(inner, (("gy", 2), ("gz", 3)), 3)
    return fold_back(beside, (2, 3))


def shards(displacement, bond_intact):
    offsets = bond_offsets()
    volume = weighted_volume()
    extent = displacement.shape[1:]
    size_x, size_y, size_z = extent
    line_x = inside_line(lax.axis_index("gx"), size_x, size_x * lax.axis_size("gx"))
    line_y = inside_line(lax.axis_index("gy"), size_y, size_y * lax.axis_size("gy"))
    line_z = inside_line(lax.axis_index("gz"), size_z, size_z * lax.axis_size("gz"))
    exists = line_x[:, None, None] * line_y[None, :, None] * line_z[None, None, :]
    anchor = (0, 0, 0)
    spread_u, fold_parts, spread_theta, fold_forces = (
        upper_displacement,
        upper_fold_parts,
        upper_dilatation,
        upper_fold_reactions,
    )
    shell_u = spread_u(displacement)
    theta_sum = jnp.zeros(exists.shape, jnp.float32)
    for bond_index, offset in enumerate(offsets):
        intact = bond_intact[bond_index].astype(jnp.float32) * window(exists, offset, extent)
        pieces, length = bond_vector(displacement, window(shell_u, offset, extent), offset)
        term = dilatation_term(length, offset, intact, volume)
        theta_sum = add_block(theta_sum, term, anchor)
        theta_sum = add_block(theta_sum, term, offset)
    theta = fold_parts(theta_sum)
    shell_theta = spread_theta(theta)
    force_sum = jnp.zeros((3,) + exists.shape, jnp.float32)
    for bond_index, offset in enumerate(offsets):
        intact = bond_intact[bond_index].astype(jnp.float32) * window(exists, offset, extent)
        pieces, length = bond_vector(displacement, window(shell_u, offset, extent), offset)
        scalar = force_scalar(
            length, offset, theta, window(shell_theta, offset, extent), intact, volume
        )
        push = jnp.stack([scalar * piece for piece in pieces])
        force_sum = add_block(force_sum, push, anchor)
        force_sum = add_block(force_sum, -push, offset)
    force = fold_forces(force_sum)
    return (force, theta)


def solution(mesh):
    return jax.shard_map(
        shards,
        mesh=mesh,
        in_specs=(P(None, "gx", "gy", "gz"), P(None, "gx", "gy", "gz")),
        out_specs=(P(None, "gx", "gy", "gz"), P("gx", "gy", "gz")),
        check_vma=False,
    )
```

profile of v0, /device:TPU:0, one launch (start us, length us, event | category | flops | bytes accessed | tf_op | source)
XLA Modules:
  0.0 1518.3 jit_solution(8872028936356348686)
XLA Ops:
  568.7 7.5 dynamic_update_slice.892
  577.2 7.5 dynamic_update_slice.893
  594.0 7.5 dynamic_update_slice.895
  610.1 7.5 dynamic_update_slice.897
  626.1 7.5 dynamic_update_slice.899
  634.5 7.5 dynamic_update_slice.900
  649.8 7.5 dynamic_update_slice.902
  666.6 7.5 dynamic_update_slice.904
  681.9 7.5 dynamic_update_slice.906
  697.2 7.5 dynamic_update_slice.908
  704.9 7.9 dynamic_update_slice.909
  712.9 7.5 dynamic_update_slice.910
  728.2 7.5 dynamic_update_slice.912
  743.5 7.5 dynamic_update_slice.914
  751.1 7.5 dynamic_update_slice.915
  766.5 7.5 dynamic_update_slice.917
  781.8 7.5 dynamic_update_slice.919
  805.7 7.5 dynamic_update_slice.922
  820.9 7.5 dynamic_update_slice.924
  843.9 7.7 dynamic_update_slice.927
  982.1 7.7 dynamic_update_slice.945
  1120.1 7.9 dynamic_update_slice.963
  1258.3 7.7 dynamic_update_slice.981
  1403.7 7.7 dynamic_update_slice.1000
  (873 shorter events, 1329.5 us)
Async XLA Ops:
  1.7 8.1 collective-permute-start.1
  3.0 7.3 collective-permute-start
  8.8 113.0 %copy-start.3 = (f32[14,14,134]{2,1,0:T(8,128)}, f32[14,14,134]{2,1,0:T(8,128)S(1)}, u32[]{:S(2)}) copy-start(f32[14,14,134]{2,1,0:T(8,128)S(1)} %broadcast_multiply_fusion) | copy-start | bytes 315172
  11.4 7.8 collective-permute-start.2
  12.7 7.7 collective-permute-start.3
  20.6 100.9 %collective-permute-start.4 = (f32[3,3,14,134]{3,2,1,0:T(8,128)S(1)}, f32[3,3,14,134]{3,2,1,0:T(8,128)S(1)}, u32[]{:S(2)}, u32[]{:S(2)}) collective-permute-start(f32[3,3,14,134]{3,2,1,0:T(8,128)S(1)} %pad_maximum_fusion.8), channel_id=1, source_target_pairs={{8,0},{16,8},{24,16},{9,1},{17,9},{25,17},{10,2},{18,10},{26,18},{... | collective-permute-start | bytes 202616 | tf_op jit(solution)/shard_map/ppermute | solution.py:29
  490.2 4.0 collective-permute-start.5
  494.2 6.2 collective-permute-start.7
  495.5 6.5 collective-permute-start.6
  502.1 7.4 collective-permute-start.9
  503.4 7.6 collective-permute-start.8
  513.7 5.9 collective-permute-start.11
  515.0 6.0 collective-permute-start.10
  521.1 7.7 collective-permute-start.12
  522.5 6.6 collective-permute-start.13
  531.9 6.7 collective-permute-start.14
  559.4 65.8 %copy-start.23 = (f32[1,8,8,128]{3,2,1,0:T(8,128)S(1)}, f32[1,8,8,128]{3,2,1,0:T(8,128)}, u32[]{:S(2)}) copy-start(f32[1,8,8,128]{3,2,1,0:T(8,128)} %get-tuple-element.508) | copy-start | bytes 98308
  576.2 65.8 %copy-start.18 = (f32[1,8,8,128]{3,2,1,0:T(8,128)S(1)}, f32[1,8,8,128]{3,2,1,0:T(8,128)}, u32[]{:S(2)}) copy-start(f32[1,8,8,128]{3,2,1,0:T(8,128)} %get-tuple-element.494) | copy-start | bytes 98308
  576.2 65.8 %copy-start.19 = (f32[1,8,8,128]{3,2,1,0:T(8,128)S(1)}, f32[1,8,8,128]{3,2,1,0:T(8,128)}, u32[]{:S(2)}) copy-start(f32[1,8,8,128]{3,2,1,0:T(8,128)} %get-tuple-element.495) | copy-start | bytes 98308
  1487.7 4.0 collective-permute-start.15
  1491.8 6.8 collective-permute-start.17
  1493.1 7.0 collective-permute-start.16
  1500.4 9.3 collective-permute-start.19
  1501.7 9.8 collective-permute-start.18
  (134 other events, 4879.1 us)
where the time goes:
time: 1540 us; the launch traced here: 1520 us
  local copies, waits for them, and re-layouts  1260 us (82%)
  other arithmetic  176 us (11%)
  starting transfers between devices  57.5 us (4%)
  waiting for transfers between devices  19.2 us (1%)
    dynamic_update_slice x244, local copies, waits for them, and re-layouts, add_block(): return lax.dynamic_update_slice(target, current + block, starts)  1250 us
    add x242, other arithmetic, add_block(): return lax.dynamic_update_slice(target, current + block, starts)  146 us
    ppermute x8, starting transfers between devices, extended_2(): before = lax.ppermute(last, axis, up)  38.2 us
  transfers between devices with their start and end apart: 20, of which 14 were waited for; matrix products, arithmetic and copies ran while one was open for 7% of the time, Pallas kernels for 0%

commit v1 on v0

v1 whole, which is shorter than its diff:
```python
import functools
import math

import jax
import jax.numpy as jnp
from jax import lax
from jax.experimental import pallas as pl
from jax.experimental.pallas import tpu as pltpu
from jax.sharding import PartitionSpec as P

MESH = pl.DeviceIdType.MESH
bulk_modulus = 150.0
shear_modulus = 25.0
soft_stretch = 0.05
PAD = 4


def bond_offsets():
    chosen = []
    for step_x in range(0, 4):
        for step_y in range(-3, 4):
            for step_z in range(-3, 4):
                if step_x * step_x + step_y * step_y + step_z * step_z > 9:
                    continue
                if step_x > 0 or (step_x == 0 and (step_y > 0 or (step_y == 0 and step_z > 0))):
                    chosen.append((step_x, step_y, step_z))
    return chosen


def square(offset):
    return sum(step * step for step in offset)


def weighted_volume():
    return 2.0 * sum(math.exp(-square(o) / 9.0) * square(o) for o in bond_offsets())


ORDER = sorted(range(len(bond_offsets())), key=lambda k: (bond_offsets()[k][:2], bond_offsets()[k][2]))


def kernel(
    sizes, u_in, intact_hbm, force_out, theta_out,
    intact, jf, ext_s, len_s, mask, u, uz, t, tz, acc_t, acc_f, main_t, main_f,
    pack_u, pack_t, edge_t, edge_f,
    zs_u, zl_u, zh_u, yu_u, yd_u, yl_u, yh_u, pu_u, pd_u, pl_u, ph_u,
    zs_t, zl_t, zh_t, yu_t, yd_t, yl_t, yh_t, pu_t, pd_t, pl_t, ph_t,
    fx_t, fxp_t, fyu_t, fyd_t, fyl_t, fyh_t, fzs_t, fzl_t, fzh_t,
    fx_f, fxp_f, fyu_f, fyd_f, fyl_f, fyh_f, fzs_f, fzl_f, fzh_f,
    send_sem, recv_sem, load_sem,
):
    offsets = bond_offsets()
    volume = weighted_volume()
    bx, by, bz = u_in.shape[1:]
    rows = by + 2 * PAD
    per = bz // 6
    index = {a: lax.axis_index(a) for a in sizes}
    has_lo = {a: index[a] > 0 for a in sizes}
    has_hi = {a: index[a] < sizes[a] - 1 for a in sizes}
    own = slice(PAD, PAD + by)
    tiles = [slice(i, i + 8) for i in range(0, rows, 8)]

    load = pltpu.make_async_copy(intact_hbm, intact, load_sem)
    load.start()

    barrier = pltpu.get_barrier_semaphore()
    count = jnp.int32(0)
    for a in sizes:
        for has, step in ((has_lo[a], -1), (has_hi[a], 1)):
            count = count + jnp.where(has, 1, 0).astype(jnp.int32)

            @pl.when(has)
            def _(a=a, step=step):
                pl.semaphore_signal(barrier, inc=1, device_id={a: index[a] + step}, device_id_type=MESH)

    used = [0]

    class Shift:
        def __init__(self, axis, step, src, dst):
            number = used[0]
            used[0] += 1
            self.copy = pltpu.make_async_remote_copy(
                src_ref=src, dst_ref=dst, send_sem=send_sem.at[number], recv_sem=recv_sem.at[number],
                device_id={axis: index[axis] + step}, device_id_type=MESH,
            )
            self.sends = has_hi[axis] if step > 0 else has_lo[axis]
            self.takes = has_lo[axis] if step > 0 else has_hi[axis]
            self.dst = dst

            @pl.when(self.sends)
            def _():
                self.copy.start()

        def receive(self):
            @pl.when(self.takes)
            def _():
                self.copy.wait_recv()

            @pl.when(jnp.logical_not(self.takes))
            def _():
                self.dst[...] = jnp.zeros(self.dst.shape, jnp.float32)

            pending.append(self)

        def finish(self):
            @pl.when(self.sends)
            def _():
                self.copy.wait_send()

    pending = []

    lane8 = lax.broadcasted_iota(jnp.int32, (8, bz), 1)
    lane = lax.broadcasted_iota(jnp.int32, (by, bz), 1)
    row = lax.broadcasted_iota(jnp.int32, (by, bz), 0)
    edge = (lane < 3) | (lane >= bz - 3)
    first = lax.rem(lane, 6) < 3

    def place(x, c, comps):
        group = x * comps + c
        return group // per, 6 * (group % per) + 3

    def roll(value, amount):
        return pltpu.roll(value, amount % bz, 1)

    def spread_a(f, comps, zs, zl, zh, yu, yd, yl, yh):
        n = zs.shape[0]
        packed = [None] * n
        for x in range(bx):
            for c in range(comps):
                value = f[x, c, own, :]
                slot, at = place(x, c, comps)
                moved = roll(jnp.where(edge, value, 0.0), at)
                packed[slot] = moved if packed[slot] is None else packed[slot] + moved
                i = x * comps + c
                part = slice(4 * (i % 2), 4 * (i % 2) + 4)
                yu[i // 2, part, :] = f[x, c, PAD + by - 4 : PAD + by, :]
                yd[i // 2, part, :] = f[x, c, PAD : PAD + 4, :]
        for s in range(n):
            zs[s] = packed[s]

    def spread_b(zs, zl, zh, yu, yd, yl, yh):
        z = Shift("gz", 1, zs, zl), Shift("gz", -1, zs, zh)
        y = Shift("gy", 1, yu, yl), Shift("gy", -1, yd, yh)
        return z, y

    def spread_c(f, comps, pack, z, y, zl, zh, yl, yh, pu, pd, plo, phi):
        n = zl.shape[0]
        for s in z:
            s.receive()
        for s in range(n):
            pack[s, own, :] = jnp.where(first, zl[s], zh[s])
            pu[s, 0:4, :] = pack[s, PAD + by - 4 : PAD + by, :]
            pd[s, 0:4, :] = pack[s, PAD : PAD + 4, :]
            pu[s, 4:8, :] = jnp.zeros((4, bz), jnp.float32)
            pd[s, 4:8, :] = jnp.zeros((4, bz), jnp.float32)
        p = Shift("gy", 1, pu, plo), Shift("gy", -1, pd, phi)
        for s in y:
            s.receive()
        for x in range(bx):
            for c in range(comps):
                i = x * comps + c
                part = slice(4 * (i % 2), 4 * (i % 2) + 4)
                f[x, c, 0:4, :] = yl[i // 2, part, :]
                f[x, c, PAD + by : rows, :] = yh[i // 2, part, :]
        xs = Shift("gx", -1, f.at[0:3], f.at[bx : bx + 3])
        for s in p:
            s.receive()
        for s in range(n):
            pack[s, 0:4, :] = plo[s, 0:4, :]
            pack[s, PAD + by : rows, :] = phi[s, 0:4, :]
        xp = Shift("gx", -1, pack.at[0], pack.at[n])
        return xs, xp

    def shifted(f, comps, pack, out, low, high):
        n = pack.shape[0] - 1
        for x in range(low, high):
            for c in range(comps):
                slot, at = place(x, c, comps) if x < bx else (n, place(x - bx, c, comps)[1])
                for tile in tiles:
                    value = f[x, c, tile, :]
                    beyond = roll(pack[slot, tile, :], -at)
                    for s in range(-3, 4):
                        if s == 0:
                            moved = value
                        else:
                            fresh = lane8 < s if s > 0 else lane8 >= bz + s
                            moved = roll(jnp.where(fresh, beyond, value), -s)
                        if comps == 3 and c == 2 and s != 0:
                            moved = moved + float(s)
                        out[s + 3, x, c, tile, :] = moved

    def combine(acc, comps, main, edges, low, high):
        n = edges.shape[0] - 1
        total = {}
        for x in range(low, high):
            for c in range(comps):
                slot, at = place(x, c, comps) if x < bx else (n, place(x - bx, c, comps)[1])
                for i, tile in enumerate(tiles):
                    inner = acc[3, x, c, tile, :]
                    over = None
                    for s in (-3, -2, -1, 1, 2, 3):
                        moved = roll(acc[s + 3, x, c, tile, :], s)
                        wrapped = lane8 < s if s > 0 else lane8 >= bz + s
                        inner = inner + jnp.where(wrapped, 0.0, moved)
                        beyond = jnp.where(wrapped, moved, 0.0)
                        over = beyond if over is None else over + beyond
                    main[x, c, tile, :] = inner
                    over = roll(over, at)
                    total[slot, i] = over if (slot, i) not in total else total[slot, i] + over
        for (slot, i), value in total.items():
            edges[slot, tiles[i], :] = value

    def fold_x(main, edges, fx, fxp):
        n = edges.shape[0] - 1
        return Shift("gx", 1, main.at[bx : bx + 3], fx), Shift("gx", 1, edges.at[n], fxp)

    def fold_y(comps, main, edges, xs, fx, fxp, fyu, fyd, fyl, fyh):
        n = edges.shape[0] - 1
        for s in xs:
            s.receive()
        for x in range(3):
            for c in range(comps):
                for tile in tiles:
                    main[x, c, tile, :] += fx[x, c, tile, :]
        for tile in tiles:
            edges[0, tile, :] += fxp[tile, :]
        base = (bx * comps + 1) // 2
        pieces = [(main.at[x, c], i) for i, (x, c) in enumerate((x, c) for x in range(bx) for c in range(comps))]
        pieces += [(edges.at[s], 2 * base + s) for s in range(n)]
        if n % 2:
            fyu[base + n // 2, 4:8, :] = jnp.zeros((4, bz), jnp.float32)
            fyd[base + n // 2, 4:8, :] = jnp.zeros((4, bz), jnp.float32)
        for ref, i in pieces:
            part = slice(4 * (i % 2), 4 * (i % 2) + 4)
            fyu[i // 2, part, :] = ref[PAD + by : rows, :]
            fyd[i // 2, part, :] = ref[0:PAD, :]
        return (Shift("gy", 1, fyu, fyl), Shift("gy", -1, fyd, fyh)), pieces

    def fold_z(pieces, edges, ys, fyl, fyh, fzs, fzl, fzh):
        n = edges.shape[0] - 1
        for s in ys:
            s.receive()
        for ref, i in pieces[-n:]:
            part = slice(4 * (i % 2), 4 * (i % 2) + 4)
            ref[PAD : PAD + 4, :] += fyl[i // 2, part, :]
            ref[PAD + by - 4 : PAD + by, :] += fyh[i // 2, part, :]
        for s in range(n):
            fzs[s] = edges[s, own, :]
        zs = Shift("gz", 1, fzs, fzl), Shift("gz", -1, fzs, fzh)
        for ref, i in pieces[:-n]:
            part = slice(4 * (i % 2), 4 * (i % 2) + 4)
            ref[PAD : PAD + 4, :] += fyl[i // 2, part, :]
            ref[PAD + by - 4 : PAD + by, :] += fyh[i // 2, part, :]
        return zs

    def fold_end(comps, main, zs, fzl, fzh, write):
        for s in zs:
            s.receive()
        arrived = [jnp.where(first, fzh[s], fzl[s]) for s in range(fzl.shape[0])]
        for x in range(bx):
            for c in range(comps):
                slot, at = place(x, c, comps)
                beyond = jnp.where(edge, roll(arrived[slot], -at), 0.0)
                write(x, c, main[x, c, own, :] + beyond)

    for x in range(bx):
        for c in range(3):
            u[x, c, own, :] = u_in[c, x]
    spread_a(u, 3, zs_u, zl_u, zh_u, yu_u, yd_u, yl_u, yh_u)
    pl.semaphore_wait(barrier, count)
    z, y = spread_b(zs_u, zl_u, zh_u, yu_u, yd_u, yl_u, yh_u)

    pairs = sorted({o[1:] for o in offsets})
    at_y = index["gy"] * by + row
    at_z = index["gz"] * bz + lane
    for i, (ey, ez) in enumerate(pairs):
        inside = (at_y + ey >= 0) & (at_y + ey < sizes["gy"] * by) & (at_z + ez >= 0) & (at_z + ez < sizes["gz"] * bz)
        mask[i] = jnp.where(inside, 1.0, 0.0)

    def clear(acc):
        zeros = jnp.zeros(acc.shape[2:], jnp.float32)

        def body(i, carry):
            for s in range(7):
                acc[s, i] = zeros
            return carry

        lax.fori_loop(0, acc.shape[1], body, 0)

    clear(acc_t)
    load.wait()

    def prepare(x, carry):
        for k in ORDER:
            ex, ey, ez = offsets[k]
            value = intact[k, x].astype(jnp.float32) * mask[pairs.index((ey, ez))]
            if ex:
                value = value * jnp.where((x + ex < bx) | has_hi["gx"], 1.0, 0.0)
            jf[k, x] = value
        return carry

    xs = spread_c(u, 3, pack_u, z, y, zl_u, zh_u, yl_u, yh_u, pu_u, pd_u, pl_u, ph_u)
    lax.fori_loop(0, bx, prepare, 0)
    shifted(u, 3, pack_u, uz, 0, bx)
    for s in xs:
        s.receive()
    shifted(u, 3, pack_u, uz, bx, bx + 3)

    def bond(x, k, mine):
        ex, ey, ez = offsets[k]
        part = slice(PAD + ey, PAD + ey + by)
        other = [uz[ez + 3, x + ex, c, part, :] for c in range(3)]
        if ex:
            other[0] = other[0] + float(ex)
        if ey:
            other[1] = other[1] + float(ey)
        return [other[c] - mine[c] for c in range(3)], part

    def dilate(x, carry):
        mine = [u[x, c, own, :] for c in range(3)]
        total = jnp.zeros((by, bz), jnp.float32)
        for k in ORDER:
            ex, ey, ez = offsets[k]
            d, part = bond(x, k, mine)
            radius = math.sqrt(square(offsets[k]))
            weight = math.exp(-square(offsets[k]) / 9.0)
            long2 = d[0] * d[0] + d[1] * d[1] + d[2] * d[2]
            ext = long2 * lax.rsqrt(long2) - radius
            term = jf[k, x] * (3.0 / volume * weight * radius) * ext
            ext_s[k, x] = ext
            len_s[k, x] = long2
            total = total + term
            acc_t[ez + 3, x + ex, 0, part, :] += term
        acc_t[3, x, 0, own, :] += total
        return carry

    lax.fori_loop(0, bx, dilate, 0)

    def soften(part):
        def body(x, carry):
            for k in part:
                radius = math.sqrt(square(offsets[k]))
                weight = math.exp(-square(offsets[k]) / 9.0)
                ext = ext_s[k, x]
                more = 1.0 + (ext * ext) * (1.0 / (radius * soft_stretch) ** 2)
                scale = jf[k, x] * lax.rsqrt(more * more * len_s[k, x])
                a = 3.0 * bulk_modulus / volume * weight * radius
                b = 15.0 * shear_modulus / volume * weight
                len_s[k, x] = scale * (a - b * radius / 3.0)
                ext_s[k, x] = scale * ext * (2.0 * b)
            return carry

        lax.fori_loop(0, bx, body, 0)

    third = (len(ORDER) + 2) // 3
    combine(acc_t, 1, main_t, edge_t, bx, bx + 3)
    xs = fold_x(main_t, edge_t, fx_t, fxp_t)
    combine(acc_t, 1, main_t, edge_t, 0, bx)
    soften(ORDER[:third])
    ys, pieces = fold_y(1, main_t, edge_t, xs, fx_t, fxp_t, fyu_t, fyd_t, fyl_t, fyh_t)
    soften(ORDER[third : 2 * third])
    zs = fold_z(pieces, edge_t, ys, fyl_t, fyh_t, fzs_t, fzl_t, fzh_t)
    soften(ORDER[2 * third :])

    def write_theta(x, c, value):
        theta_out[x] = value
        t[x, 0, own, :] = value

    fold_end(1, main_t, zs, fzl_t, fzh_t, write_theta)
    spread_a(t, 1, zs_t, zl_t, zh_t, yu_t, yd_t, yl_t, yh_t)
    z, y = spread_b(zs_t, zl_t, zh_t, yu_t, yd_t, yl_t, yh_t)
    clear(acc_f)
    xs = spread_c(t, 1, pack_t, z, y, zl_t, zh_t, yl_t, yh_t, pu_t, pd_t, pl_t, ph_t)
    shifted(t, 1, pack_t, tz, 0, bx)
    for s in xs:
        s.receive()
    shifted(t, 1, pack_t, tz, bx, bx + 3)

    def push(x, carry):
        mine = [u[x, c, own, :] for c in range(3)]
        here = t[x, 0, own, :]
        total = [jnp.zeros((by, bz), jnp.float32) for c in range(3)]
        for k in ORDER:
            ex, ey, ez = offsets[k]
            d, part = bond(x, k, mine)
            scalar = len_s[k, x] * (here + tz[ez + 3, x + ex, 0, part, :]) + ext_s[k, x]
            for c in range(3):
                pushed = scalar * d[c]
                total[c] = total[c] + pushed
                acc_f[ez + 3, x + ex, c, part, :] -= pushed
        for c in range(3):
            acc_f[3, x, c, own, :] += total[c]
        return carry

    lax.fori_loop(0, bx, push, 0)
    combine(acc_f, 3, main_f, edge_f, bx, bx + 3)
    xs = fold_x(main_f, edge_f, fx_f, fxp_f)
    combine(acc_f, 3, main_f, edge_f, 0, bx)
    ys, pieces = fold_y(3, main_f, edge_f, xs, fx_f, fxp_f, fyu_f, fyd_f, fyl_f, fyh_f)
    zs = fold_z(pieces, edge_f, ys, fyl_f, fyh_f, fzs_f, fzl_f, fzh_f)

    def write_force(x, c, value):
        force_out[c, x] = value

    fold_end(3, main_f, zs, fzl_f, fzh_f, write_force)
    for s in pending:
        s.finish()


def shards(sizes, displacement, bond_intact):
    bx, by, bz = displacement.shape[1:]
    bonds = bond_intact.shape[0]
    rows = by + 2 * PAD
    f32 = lambda *shape: pltpu.VMEM(shape, jnp.float32)
    slots = {c: -(-bx * c // (bz // 6)) for c in (1, 3)}

    def spread_buffers(c):
        n, m = slots[c], (bx * c + 1) // 2
        return [f32(n, by, bz)] * 3 + [f32(m, 8, bz)] * 4 + [f32(n, 8, bz)] * 4

    def fold_buffers(c):
        n, m = slots[c], (bx * c + 1) // 2
        return (
            [f32(3, c, rows, bz), f32(rows, bz)]
            + [f32(m + (n + 1) // 2, 8, bz)] * 4
            + [f32(n, by, bz)] * 3
        )

    pairs = len({o[1:] for o in bond_offsets()})
    scratch = (
        [pltpu.VMEM((bonds, bx, by, bz), jnp.int32)]
        + [f32(bonds, bx, by, bz)] * 3
        + [f32(pairs, by, bz)]
        + [f32(bx + 3, 3, rows, bz), f32(7, bx + 3, 3, rows, bz)]
        + [f32(bx + 3, 1, rows, bz), f32(7, bx + 3, 1, rows, bz)]
        + [f32(7, bx + 3, 1, rows, bz), f32(7, bx + 3, 3, rows, bz)]
        + [f32(bx + 3, 1, rows, bz), f32(bx + 3, 3, rows, bz)]
        + [f32(slots[3] + 1, rows, bz), f32(slots[1] + 1, rows, bz)]
        + [f32(slots[1] + 1, rows, bz), f32(slots[3] + 1, rows, bz)]
        + spread_buffers(3) + spread_buffers(1) + fold_buffers(1) + fold_buffers(3)
        + [pltpu.SemaphoreType.DMA((28,)), pltpu.SemaphoreType.DMA((28,)), pltpu.SemaphoreType.DMA]
    )
    vmem = pl.BlockSpec(memory_space=pltpu.VMEM)
    return pl.pallas_call(
        functools.partial(kernel, sizes),
        out_shape=(
            jax.ShapeDtypeStruct(displacement.shape, jnp.float32),
            jax.ShapeDtypeStruct(displacement.shape[1:], jnp.float32),
        ),
        in_specs=[vmem, pl.BlockSpec(memory_space=pl.ANY)],
        out_specs=(vmem, vmem),
        scratch_shapes=scratch,
        compiler_params=pltpu.CompilerParams(collective_id=0, has_side_effects=True, vmem_limit_bytes=40 << 20),
    )(displacement, bond_intact)


def solution(mesh):
    sizes = {a: mesh.shape[a] for a in ("gx", "gy", "gz")}
    return jax.shard_map(
        functools.partial(shards, sizes),
        mesh=mesh,
        in_specs=(P(None, "gx", "gy", "gz"), P(None, "gx", "gy", "gz")),
        out_specs=(P(None, "gx", "gy", "gz"), P("gx", "gy", "gz")),
        check_vma=False,
    )
```

time: 1540 us -> 44.6 us (0.03)
  the two profiles are of different devices: /device:TPU:0 before, /device:TPU:2 now
where the time goes in v1:
time: 44.6 us; the launch traced here: 44.5 us
  Pallas kernels  40.1 us (90%)
  local copies, waits for them, and re-layouts  3.7 us (8%)
  between operations  0.65 us (1%)
    pallas_call x1, Pallas kernels, shards(): pl.pallas_call(functools.partial(kernel, sizes), out_shape=(jax.ShapeDtyp...  40.1 us
    unnamed x6, local copies, waits for them, and re-layouts  3.7 us

profile of v1, /device:TPU:2, one launch (start us, length us, event | category | flops | bytes accessed | tf_op | source)
XLA Modules:
  0.0 44.5 jit_solution(7623264248536551528)
XLA Ops:
  0.6 0.0 copy-start
  0.6 1.5 %copy-done = s32[61,8,8,128]{3,2,1,0:T(8,128)S(1)} copy-done((s32[61,8,8,128]{3,2,1,0:T(8,128)S(1)}, s32[61,8,8,128]{3,2,1,0:T(8,128)}, u32[]{:S(2)}) %copy-start) | copy-done | bytes 1998872
  2.2 0.0 copy-start.1
  2.2 0.9 %copy-done.1 = f32[3,8,8,128]{3,2,1,0:T(8,128)S(1)} copy-done((f32[3,8,8,128]{3,2,1,0:T(8,128)S(1)}, f32[3,8,8,128]{3,2,1,0:T(8,128)}, u32[]{:S(2)}) %copy-start.1) | copy-done | bytes 98328
  3.1 40.1 %shard_map.41 = (f32[3,8,8,128]{3,2,1,0:T(8,128)S(1)}, f32[8,8,128]{2,1,0:T(8,128)S(1)}) custom-call(f32[3,8,8,128]{3,2,1,0:T(8,128)S(1)} %copy-done.1, s32[61,8,8,128]{3,2,1,0:T(8,128)S(1)} %copy-done), custom_call_target="tpu_custom_call" | custom-call | tf_op jit(solution)/shard_map/pallas_call | solution.py:443
  43.2 0.6 %copy.6 = f32[3,8,8,128]{3,2,1,0:T(8,128)} copy(f32[3,8,8,128]{3,2,1,0:T(8,128)S(1)} %get-tuple-element.4) | data formatting | bytes 196608
  43.8 0.6 %copy.7 = f32[8,8,128]{2,1,0:T(8,128)} copy(f32[8,8,128]{2,1,0:T(8,128)S(1)} %get-tuple-element.5) | data formatting | bytes 65536
Async XLA Ops:
  0.6 1.6 %copy-start = (s32[61,8,8,128]{3,2,1,0:T(8,128)S(1)}, s32[61,8,8,128]{3,2,1,0:T(8,128)}, u32[]{:S(2)}) copy-start(s32[61,8,8,128]{3,2,1,0:T(8,128)} %intact_hbm.1) | copy-start | bytes 5996548
  2.2 0.9 %copy-start.1 = (f32[3,8,8,128]{3,2,1,0:T(8,128)S(1)}, f32[3,8,8,128]{3,2,1,0:T(8,128)}, u32[]{:S(2)}) copy-start(f32[3,8,8,128]{3,2,1,0:T(8,128)} %u_in.1) | copy-start | bytes 294916

commit v2 on v1

v2 whole, which is shorter than its diff:
```python
import functools
import math

import jax
import jax.numpy as jnp
from jax import lax
from jax.experimental import pallas as pl
from jax.experimental.pallas import tpu as pltpu
from jax.sharding import PartitionSpec as P

MESH = pl.DeviceIdType.MESH
bulk_modulus = 150.0
shear_modulus = 25.0
soft_stretch = 0.05
PAD = 4


def bond_offsets():
    chosen = []
    for step_x in range(0, 4):
        for step_y in range(-3, 4):
            for step_z in range(-3, 4):
                if step_x * step_x + step_y * step_y + step_z * step_z > 9:
                    continue
                if step_x > 0 or (step_x == 0 and (step_y > 0 or (step_y == 0 and step_z > 0))):
                    chosen.append((step_x, step_y, step_z))
    return chosen


def square(offset):
    return sum(step * step for step in offset)


def weighted_volume():
    return 2.0 * sum(math.exp(-square(o) / 9.0) * square(o) for o in bond_offsets())


ORDER = sorted(range(len(bond_offsets())), key=lambda k: (bond_offsets()[k][:2], bond_offsets()[k][2]))


def spread_parts(c, bx, by, bz):
    n, m, mx = -(-bx * c // (bz // 6)), (bx * c + 1) // 2, (3 * c + 1) // 2
    sent = {"z": (n, by, bz), "y+": (m, 8, bz), "y-": (m, 8, bz), "c+": (n, 8, bz), "c-": (n, 8, bz)}
    taken = {}
    for dy in (-1, 0, 1):
        for dz in (-1, 0, 1):
            shape = ((c, 3, by, bz), (1, by, bz), (mx, 8, bz), (1, 8, bz))[2 * abs(dy) + abs(dz)]
            taken[1, dy, dz] = shape
            if dy or dz:
                taken[0, dy, dz] = (None, (n, by, bz), (m, 8, bz), (n, 8, bz))[2 * abs(dy) + abs(dz)]
    return sent, taken


def fold_sent(c, bx, by, bz):
    sent, taken = spread_parts(c, bx, by, bz)
    sent["x"], sent["xz"] = (c, 3, by, bz), (1, by, bz)
    for sign, dy in (("+", 1), ("-", -1)):
        sent["xy" + sign], sent["xc" + sign] = taken[1, dy, 0], taken[1, dy, 1]
    return sent


def scratch_plan(bonds, bx, by, bz):
    rows = by + 2 * PAD
    pairs = len({o[1:] for o in bond_offsets()})
    plan = {"jf": (bonds, bx, by, bz), "ext": (bonds, bx, by, bz), "len": (bonds, bx, by, bz), "mask": (pairs, by, bz)}
    plan["u_in"] = (3, bx, by, bz)
    for name, c in (("u", 3), ("t", 1)):
        sent, taken = spread_parts(c, bx, by, bz)
        n = sent["z"][0]
        plan[name, "field"] = (bx + 3, c, rows, bz)
        plan[name, "shifted"] = plan[name, "sums"] = (7, bx + 3, c, rows, bz)
        plan[name, "main"] = (bx + 3, c, rows, bz)
        plan[name, "pack"] = plan[name, "edges"] = (n + 1, rows, bz)
        for key, shape in sent.items():
            plan[name, "s", key] = shape
        for key, shape in fold_sent(c, bx, by, bz).items():
            plan[name, "fs", key] = shape
        for key, shape in taken.items():
            plan[name, "r", key] = shape
            plan[name, "fr", key] = shape
    return plan


def kernel(sizes, names, u_hbm, intact_hbm, force_out, theta_out, *scratch):
    B = dict(zip(names, scratch))
    intact, send_sem, recv_sem, load_sem = scratch[len(names) :]
    offsets = bond_offsets()
    volume = weighted_volume()
    bx, by, bz = theta_out.shape
    rows = by + 2 * PAD
    per = bz // 6
    axes = ("gx", "gy", "gz")
    index = {a: lax.axis_index(a) for a in axes}
    has = {(a, -1): index[a] > 0 for a in axes}
    has.update({(a, 1): index[a] < sizes[a] - 1 for a in axes})
    own = slice(PAD, PAD + by)
    below, above = slice(0, PAD), slice(PAD + by, rows)
    tiles = [slice(i, i + 8) for i in range(0, rows, 8)]
    jf, ext_s, len_s, mask = B["jf"], B["ext"], B["len"], B["mask"]

    def there(direction):
        found = None
        for a, step in zip(axes, direction):
            if step:
                found = has[a, step] if found is None else found & has[a, step]
        return found

    everyone = [(x, y, z) for x in (-1, 0, 1) for y in (-1, 0, 1) for z in (-1, 0, 1) if x or y or z]
    exists = {d: there(d) for d in everyone}

    def device(direction):
        return {a: index[a] + step for a, step in zip(axes, direction) if step}

    load_u = pltpu.make_async_copy(u_hbm, B["u_in"], load_sem.at[0])
    load_u.start()
    load = pltpu.make_async_copy(intact_hbm, intact, load_sem.at[1])
    load.start()
    for key, ref in B.items():
        if isinstance(key, tuple) and key[1] in ("r", "fr"):
            ref[...] = jnp.zeros(ref.shape, jnp.float32)

    barrier = pltpu.get_barrier_semaphore()
    count = jnp.int32(0)
    for d in everyone:
        count = count + jnp.where(exists[d], 1, 0).astype(jnp.int32)

        @pl.when(exists[d])
        def _(d=d):
            pl.semaphore_signal(barrier, inc=1, device_id=device(d), device_id_type=MESH)

    copies = []

    class Shift:
        def __init__(self, direction, src, dst):
            number = len(copies)
            copies.append(self)
            self.copy = pltpu.make_async_remote_copy(
                src_ref=src, dst_ref=dst, send_sem=send_sem.at[number], recv_sem=recv_sem.at[number],
                device_id=device(direction), device_id_type=MESH,
            )
            self.sends = exists[direction]
            self.takes = exists[tuple(-step for step in direction)]

            @pl.when(self.sends)
            def _():
                self.copy.start()

        def receive(self):
            @pl.when(self.takes)
            def _():
                self.copy.wait_recv()

        def finish(self):
            @pl.when(self.sends)
            def _():
                self.copy.wait_send()

    lane8 = lax.broadcasted_iota(jnp.int32, (8, bz), 1)
    lane = lax.broadcasted_iota(jnp.int32, (by, bz), 1)
    row = lax.broadcasted_iota(jnp.int32, (by, bz), 0)
    edge = (lane < 3) | (lane >= bz - 3)
    first = lax.rem(lane, 6) < 3
    first4 = lax.rem(lax.broadcasted_iota(jnp.int32, (4, bz), 1), 6) < 3
    zeros4 = jnp.zeros((4, bz), jnp.float32)

    def place(x, c, comps):
        group = x % bx * comps + c
        return group // per, 6 * (group % per) + 3

    def half(i):
        return slice(4 * (i % 2), 4 * (i % 2) + 4)

    def roll(value, amount):
        return pltpu.roll(value, amount % bz, 1)

    def planes(comps, low, high):
        return [(x, c) for x in range(low, high) for c in range(comps)]

    signs = (("+", 1), ("-", -1))

    def spread(name, comps, whole):
        field = B[name, "field"]
        z = B[name, "s", "z"]
        n = z.shape[0]
        mx = (3 * comps + 1) // 2
        packed = [None] * n
        for i, (x, c) in enumerate(planes(comps, 0, bx)):
            slot, at = place(x, c, comps)
            moved = roll(jnp.where(edge, field[x, c, own, :], 0.0), at)
            packed[slot] = moved if packed[slot] is None else packed[slot] + moved
            B[name, "s", "y+"][i // 2, half(i), :] = field[x, c, PAD + by - 4 : PAD + by, :]
            B[name, "s", "y-"][i // 2, half(i), :] = field[x, c, PAD : PAD + 4, :]
        for s in range(n):
            z[s] = packed[s]
            B[name, "s", "c+"][s, 0:4, :] = z[s, by - 4 : by, :]
            B[name, "s", "c-"][s, 0:4, :] = z[s, 0:4, :]
            B[name, "s", "c+"][s, 4:8, :] = zeros4
            B[name, "s", "c-"][s, 4:8, :] = zeros4
        return mx, whole

    def spread_send(name, mx, whole):
        sent = {}
        for far in (1, 0):
            for dy in (1, -1, 0):
                for dz in (1, -1, 0):
                    if (far, dy, dz) == (0, 0, 0):
                        continue
                    sign = "+" if dy > 0 else "-"
                    if dy and dz:
                        src = B[name, "s", "c" + sign]
                        src = src.at[0:1] if far else src
                    elif dy:
                        src = B[name, "s", "y" + sign]
                        src = src.at[0:mx] if far else src
                    elif dz:
                        src = B[name, "s", "z"]
                        src = src.at[0:1] if far else src
                    else:
                        src = whole
                    sent[far, dy, dz] = Shift((-far, dy, dz), src, B[name, "r", (far, dy, dz)])
        return sent

    def spread_take(name, comps, sent, far):
        for (f, dy, dz), copy in sent.items():
            if f == far:
                copy.receive()
        field, pack = B[name, "field"], B[name, "pack"]
        n = pack.shape[0] - 1
        R = lambda dy, dz: B[name, "r", (far, dy, dz)]
        for s in range(1 if far else n):
            to = n if far else s
            pack[to, own, :] = jnp.where(first, R(0, 1)[s], R(0, -1)[s])
            pack[to, below, :] = jnp.where(first4, R(1, 1)[s, 0:4, :], R(1, -1)[s, 0:4, :])
            pack[to, above, :] = jnp.where(first4, R(-1, 1)[s, 0:4, :], R(-1, -1)[s, 0:4, :])
        for i, (x, c) in enumerate(planes(comps, 0, 3 if far else bx)):
            to = x + bx if far else x
            if far:
                field[to, c, own, :] = R(0, 0)[c, x]
            field[to, c, below, :] = R(1, 0)[i // 2, half(i), :]
            field[to, c, above, :] = R(-1, 0)[i // 2, half(i), :]
        shifted(name, comps, *((bx, bx + 3) if far else (0, bx)))

    def shifted(name, comps, low, high):
        field, pack, out = B[name, "field"], B[name, "pack"], B[name, "shifted"]
        n = pack.shape[0] - 1
        for x, c in planes(comps, low, high):
            slot, at = place(x, c, comps)
            slot = slot if x < bx else n
            for tile in tiles:
                value = field[x, c, tile, :]
                beyond = roll(pack[slot, tile, :], -at)
                for s in range(-3, 4):
                    if s == 0:
                        moved = value
                    else:
                        fresh = lane8 < s if s > 0 else lane8 >= bz + s
                        moved = roll(jnp.where(fresh, beyond, value), -s)
                    if comps == 3 and c == 2 and s != 0:
                        moved = moved + float(s)
                    out[s + 3, x, c, tile, :] = moved

    def combine(name, comps, low, high):
        sums, main, edges = B[name, "sums"], B[name, "main"], B[name, "edges"]
        n = edges.shape[0] - 1
        total = {}
        for x, c in planes(comps, low, high):
            slot, at = place(x, c, comps)
            slot = slot if x < bx else n
            for i, tile in enumerate(tiles):
                inner = sums[3, x, c, tile, :]
                over = None
                for s in (-3, -2, -1, 1, 2, 3):
                    moved = roll(sums[s + 3, x, c, tile, :], s)
                    wrapped = lane8 < s if s > 0 else lane8 >= bz + s
                    inner = inner + jnp.where(wrapped, 0.0, moved)
                    beyond = jnp.where(wrapped, moved, 0.0)
                    over = beyond if over is None else over + beyond
                main[x, c, tile, :] = inner
                over = roll(over, at)
                total[slot, i] = over if (slot, i) not in total else total[slot, i] + over
        for (slot, i), value in total.items():
            edges[slot, tiles[i], :] = value

    def fold_send(name, comps, far):
        combine(name, comps, *((bx, bx + 3) if far else (0, bx)))
        main, edges = B[name, "main"], B[name, "edges"]
        n = edges.shape[0] - 1
        S = lambda key: B[name, "fs", ("x" + key) if far else key]
        for i, (x, c) in enumerate(planes(comps, 0, 3 if far else bx)):
            at = x + bx if far else x
            if far:
                B[name, "fs", "x"][c, x] = main[at, c, own, :]
            S("y+")[i // 2, half(i), :] = main[at, c, above, :]
            S("y-")[i // 2, half(i), :] = main[at, c, below, :]
        if (comps * (3 if far else bx)) % 2:
            for sign, _ in signs:
                S("y" + sign)[S("y" + sign).shape[0] - 1, 4:8, :] = zeros4
        for s in range(1 if far else n):
            at = n if far else s
            S("z")[s] = edges[at, own, :]
            S("c+")[s, 0:4, :] = edges[at, above, :]
            S("c-")[s, 0:4, :] = edges[at, below, :]
            S("c+")[s, 4:8, :] = zeros4
            S("c-")[s, 4:8, :] = zeros4
        sent = []
        for dy in (1, -1, 0):
            for dz in (1, -1, 0):
                if not (far or dy or dz):
                    continue
                sign = "+" if dy > 0 else "-"
                src = S("c" + sign) if dy and dz else S("y" + sign) if dy else S("z") if dz else B[name, "fs", "x"]
                sent.append(Shift((far, dy, dz), src, B[name, "fr", (far, dy, dz)]))
        return sent

    def fold_take(name, comps, sent, write):
        main = B[name, "main"]
        R = lambda far, dy, dz: B[name, "fr", (far, dy, dz)]
        for copy in sent:
            copy.receive()
        work = B[name, "edges"]
        n = work.shape[0] - 1
        for far in (0, 1):
            for s in range(1 if far else n):
                value = jnp.where(first, R(far, 0, -1)[s], R(far, 0, 1)[s])
                work[s, own, :] = work[s, own, :] + value if far else value
                work[s, PAD : PAD + 4, :] += jnp.where(first4, R(far, 1, -1)[s, 0:4, :], R(far, 1, 1)[s, 0:4, :])
                work[s, PAD + by - 4 : PAD + by, :] += jnp.where(
                    first4, R(far, -1, -1)[s, 0:4, :], R(far, -1, 1)[s, 0:4, :]
                )
        for i, (x, c) in enumerate(planes(comps, 0, bx)):
            upper, lower = R(0, 1, 0)[i // 2, half(i), :], R(0, -1, 0)[i // 2, half(i), :]
            if x < 3:
                upper = upper + R(1, 1, 0)[i // 2, half(i), :]
                lower = lower + R(1, -1, 0)[i // 2, half(i), :]
            main[x, c, PAD : PAD + 4, :] += upper
            main[x, c, PAD + by - 4 : PAD + by, :] += lower
        for x, c in planes(comps, 0, bx):
            slot, at = place(x, c, comps)
            value = main[x, c, own, :] + jnp.where(edge, roll(work[slot, own, :], -at), 0.0)
            if x < 3:
                value = value + R(1, 0, 0)[c, x]
            write(x, c, value)

    u, uz, t, tz = B["u", "field"], B["u", "shifted"], B["t", "field"], B["t", "shifted"]
    acc_t, acc_f = B["t", "sums"], B["u", "sums"]
    load_u.wait()
    for x, c in planes(3, 0, bx):
        u[x, c, own, :] = B["u_in"][c, x]
    mx, whole = spread("u", 3, B["u_in"].at[:, 0:3])
    pl.semaphore_wait(barrier, count)
    sent = spread_send("u", mx, whole)

    pairs = sorted({o[1:] for o in offsets})
    at_y = index["gy"] * by + row
    at_z = index["gz"] * bz + lane
    for i, (ey, ez) in enumerate(pairs):
        inside = (at_y + ey >= 0) & (at_y + ey < sizes["gy"] * by) & (at_z + ez >= 0) & (at_z + ez < sizes["gz"] * bz)
        mask[i] = jnp.where(inside, 1.0, 0.0)

    def clear(acc):
        zeros = jnp.zeros(acc.shape[2:], jnp.float32)

        def body(i, carry):
            for s in range(7):
                acc[s, i] = zeros
            return carry

        lax.fori_loop(0, acc.shape[1], body, 0)

    clear(acc_t)
    load.wait()

    def prepare(x, carry):
        for k in ORDER:
            ex, ey, ez = offsets[k]
            value = intact[k, x].astype(jnp.float32) * mask[pairs.index((ey, ez))]
            if ex:
                value = value * jnp.where((x + ex < bx) | has["gx", 1], 1.0, 0.0)
            jf[k, x] = value
        return carry

    lax.fori_loop(0, bx, prepare, 0)
    clear(acc_f)
    spread_take("u", 3, sent, 0)
    spread_take("u", 3, sent, 1)

    def bond(x, k, mine):
        ex, ey, ez = offsets[k]
        part = slice(PAD + ey, PAD + ey + by)
        other = [uz[ez + 3, x + ex, c, part, :] for c in range(3)]
        if ex:
            other[0] = other[0] + float(ex)
        if ey:
            other[1] = other[1] + float(ey)
        return [other[c] - mine[c] for c in range(3)], part

    def dilate(x, carry):
        mine = [u[x, c, own, :] for c in range(3)]
        total = jnp.zeros((by, bz), jnp.float32)
        for k in ORDER:
            ex, ey, ez = offsets[k]
            d, part = bond(x, k, mine)
            radius = math.sqrt(square(offsets[k]))
            weight = math.exp(-square(offsets[k]) / 9.0)
            long2 = d[0] * d[0] + d[1] * d[1] + d[2] * d[2]
            ext = long2 * lax.rsqrt(long2) - radius
            term = jf[k, x] * (3.0 / volume * weight * radius) * ext
            ext_s[k, x] = ext
            len_s[k, x] = long2
            total = total + term
            acc_t[ez + 3, x + ex, 0, part, :] += term
        acc_t[3, x, 0, own, :] += total
        return carry

    lax.fori_loop(0, bx, dilate, 0)

    def soften(part):
        def body(x, carry):
            for k in part:
                radius = math.sqrt(square(offsets[k]))
                weight = math.exp(-square(offsets[k]) / 9.0)
                ext = ext_s[k, x]
                more = 1.0 + (ext * ext) * (1.0 / (radius * soft_stretch) ** 2)
                scale = jf[k, x] * lax.rsqrt(more * more * len_s[k, x])
                a = 3.0 * bulk_modulus / volume * weight * radius
                b = 15.0 * shear_modulus / volume * weight
                len_s[k, x] = scale * (a - b * radius / 3.0)
                ext_s[k, x] = scale * ext * (2.0 * b)
            return carry

        lax.fori_loop(0, bx, body, 0)

    cut = (2 * len(ORDER)) // 3
    sent = fold_send("t", 1, 1)
    sent += fold_send("t", 1, 0)
    soften(ORDER[:cut])

    def write_theta(x, c, value):
        theta_out[x] = value
        B["t_own"][0, x] = value
        t[x, 0, own, :] = value

    fold_take("t", 1, sent, write_theta)
    mx, whole = spread("t", 1, B["t_own"].at[:, 0:3])
    sent = spread_send("t", mx, whole)
    soften(ORDER[cut:])
    spread_take("t", 1, sent, 0)
    spread_take("t", 1, sent, 1)

    def push(x, carry):
        mine = [u[x, c, own, :] for c in range(3)]
        here = t[x, 0, own, :]
        total = [jnp.zeros((by, bz), jnp.float32) for c in range(3)]
        for k in ORDER:
            ex, ey, ez = offsets[k]
            d, part = bond(x, k, mine)
            scalar = len_s[k, x] * (here + tz[ez + 3, x + ex, 0, part, :]) + ext_s[k, x]
            for c in range(3):
                pushed = scalar * d[c]
                total[c] = total[c] + pushed
                acc_f[ez + 3, x + ex, c, part, :] -= pushed
        for c in range(3):
            acc_f[3, x, c, own, :] += total[c]
        return carry

    lax.fori_loop(0, bx, push, 0)
    sent = fold_send("u", 3, 1)
    sent += fold_send("u", 3, 0)

    def write_force(x, c, value):
        force_out[c, x] = value

    fold_take("u", 3, sent, write_force)
    for copy in copies:
        copy.finish()


def shards(sizes, displacement, bond_intact):
    plan = scratch_plan(bond_intact.shape[0], *displacement.shape[1:])
    plan["t_own"] = (1,) + displacement.shape[1:]
    scratch = [pltpu.VMEM(shape, jnp.float32) for shape in plan.values()]
    scratch += [
        pltpu.VMEM(bond_intact.shape, jnp.int32),
        pltpu.SemaphoreType.DMA((68,)),
        pltpu.SemaphoreType.DMA((68,)),
        pltpu.SemaphoreType.DMA((2,)),
    ]
    vmem, anywhere = pl.BlockSpec(memory_space=pltpu.VMEM), pl.BlockSpec(memory_space=pl.ANY)
    return pl.pallas_call(
        functools.partial(kernel, sizes, tuple(plan)),
        out_shape=(
            jax.ShapeDtypeStruct(displacement.shape, jnp.float32),
            jax.ShapeDtypeStruct(displacement.shape[1:], jnp.float32),
        ),
        in_specs=[anywhere, anywhere],
        out_specs=(vmem, vmem),
        scratch_shapes=scratch,
        compiler_params=pltpu.CompilerParams(collective_id=0, has_side_effects=True, vmem_limit_bytes=63 << 20),
    )(displacement, bond_intact)


def solution(mesh):
    sizes = {a: mesh.shape[a] for a in ("gx", "gy", "gz")}
    return jax.shard_map(
        functools.partial(shards, sizes),
        mesh=mesh,
        in_specs=(P(None, "gx", "gy", "gz"), P(None, "gx", "gy", "gz")),
        out_specs=(P(None, "gx", "gy", "gz"), P("gx", "gy", "gz")),
        check_vma=False,
    )
```

time: 44.6 us -> 33.8 us (0.76)
  the two profiles are of different devices: /device:TPU:2 before, /device:TPU:0 now
where the time goes in v2:
time: 33.8 us; the launch traced here: 33.6 us
  Pallas kernels  30 us (89%)
  local copies, waits for them, and re-layouts  2.91 us (9%)
  between operations  0.64 us (2%)
    pallas_call x1, Pallas kernels, shards(): pl.pallas_call(functools.partial(kernel, sizes, tuple(plan)), out_shape=(...  30 us
    unnamed x2, local copies, waits for them, and re-layouts  2.91 us

profile of v2, /device:TPU:0, one launch (start us, length us, event | category | flops | bytes accessed | tf_op | source)
XLA Modules:
  0.0 33.6 jit_solution(14656918710260093908)
XLA Ops:
  0.6 30.0 %shard_map.41 = (f32[3,8,8,128]{3,2,1,0:T(8,128)}, f32[8,8,128]{2,1,0:T(8,128)}) custom-call(f32[3,8,8,128]{3,2,1,0:T(8,128)} %u_hbm.1, s32[61,8,8,128]{3,2,1,0:T(8,128)} %intact_hbm.1), custom_call_target="tpu_custom_call" | custom-call | tf_op jit(solution)/shard_map/pallas_call | solution.py:489
  30.7 1.5 %copy.6 = f32[3,8,8,128]{3,2,1,0:T(8,128)} copy(f32[3,8,8,128]{3,2,1,0:T(8,128)} %get-tuple-element.4) | data formatting | bytes 196608
  32.2 1.4 %copy.7 = f32[8,8,128]{2,1,0:T(8,128)} copy(f32[8,8,128]{2,1,0:T(8,128)} %get-tuple-element.5) | data formatting | bytes 65536

commit v3 on v2

--- a/solution.py
+++ b/solution.py
@@ -412,7 +412,11 @@
         acc_t[3, x, 0, own, :] += total
         return carry
 
-    lax.fori_loop(0, bx, dilate, 0)
+    def sweep(work, name, comps):
+        lax.fori_loop(0, 3, lambda i, carry: work(bx - 1 - i, carry), 0)
+        sent = fold_send(name, comps, 1)
+        lax.fori_loop(0, bx - 3, lambda i, carry: work(bx - 4 - i, carry), 0)
+        return sent + fold_send(name, comps, 0)
 
     def soften(part):
         def body(x, carry):
@@ -431,8 +435,7 @@
         lax.fori_loop(0, bx, body, 0)
 
     cut = (2 * len(ORDER)) // 3
-    sent = fold_send("t", 1, 1)
-    sent += fold_send("t", 1, 0)
+    sent = sweep(dilate, "t", 1)
     soften(ORDER[:cut])
 
     def write_theta(x, c, value):
@@ -463,9 +466,7 @@
             acc_f[3, x, c, own, :] += total[c]
         return carry
 
-    lax.fori_loop(0, bx, push, 0)
-    sent = fold_send("u", 3, 1)
-    sent += fold_send("u", 3, 0)
+    sent = sweep(push, "u", 3)
 
     def write_force(x, c, value):
         force_out[c, x] = value

time: 33.8 us -> 33.9 us (level)
  no operation moved by 1% of the time
where the time goes in v3:
time: 33.9 us; the launch traced here: 33.7 us
  Pallas kernels  30.1 us (89%)
  local copies, waits for them, and re-layouts  2.91 us (9%)
  between operations  0.64 us (2%)
    pallas_call x1, Pallas kernels, shards(): pl.pallas_call(functools.partial(kernel, sizes, tuple(plan)), out_shape=(...  30.1 us
    unnamed x2, local copies, waits for them, and re-layouts  2.91 us

profile of v3, /device:TPU:0, one launch (start us, length us, event | category | flops | bytes accessed | tf_op | source)
XLA Modules:
  0.0 33.7 jit_solution(15938275348901710509)
XLA Ops:
  0.6 30.1 %shard_map.41 = (f32[3,8,8,128]{3,2,1,0:T(8,128)}, f32[8,8,128]{2,1,0:T(8,128)}) custom-call(f32[3,8,8,128]{3,2,1,0:T(8,128)} %u_hbm.1, s32[61,8,8,128]{3,2,1,0:T(8,128)} %intact_hbm.1), custom_call_target="tpu_custom_call" | custom-call | tf_op jit(solution)/shard_map/pallas_call | solution.py:490
  30.8 1.5 %copy.6 = f32[3,8,8,128]{3,2,1,0:T(8,128)} copy(f32[3,8,8,128]{3,2,1,0:T(8,128)} %get-tuple-element.4) | data formatting | bytes 196608
  32.3 1.4 %copy.7 = f32[8,8,128]{2,1,0:T(8,128)} copy(f32[8,8,128]{2,1,0:T(8,128)} %get-tuple-element.5) | data formatting | bytes 65536

commit v4 on v3

--- a/solution.py
+++ b/solution.py
@@ -496,7 +496,7 @@
         in_specs=[anywhere, anywhere],
         out_specs=(vmem, vmem),
         scratch_shapes=scratch,
-        compiler_params=pltpu.CompilerParams(collective_id=0, has_side_effects=True, vmem_limit_bytes=63 << 20),
+        compiler_params=pltpu.CompilerParams(collective_id=0, has_side_effects=True, vmem_limit_bytes=56000000),
     )(displacement, bond_intact)
 
 

time: 33.9 us -> 32.5 us (0.959)
  local copies, waits for them, and re-layouts: 2.91 us -> 2.14 us
  Pallas kernels: 30.1 us -> 29.5 us
    unnamed x2 -> x4, local copies, waits for them, and re-layouts: 2.91 us -> 2.14 us
    pallas_call x1, Pallas kernels: 30.1 us -> 29.5 us  [shards(): pl.pallas_call(functools.partial(kernel, sizes, tuple(plan)), out_shape=(...]
where the time goes in v4:
time: 32.5 us; the launch traced here: 32.3 us
  Pallas kernels  29.5 us (91%)
  local copies, waits for them, and re-layouts  2.14 us (7%)
  between operations  0.65 us (2%)
    pallas_call x1, Pallas kernels, shards(): pl.pallas_call(functools.partial(kernel, sizes, tuple(plan)), out_shape=(...  29.5 us
    unnamed x4, local copies, waits for them, and re-layouts  2.14 us

profile of v4, /device:TPU:0, one launch (start us, length us, event | category | flops | bytes accessed | tf_op | source)
XLA Modules:
  0.0 32.3 jit_solution(16167824370692166222)
XLA Ops:
  0.6 0.0 copy-start
  0.6 0.9 %copy-done = f32[3,8,8,128]{3,2,1,0:T(8,128)S(1)} copy-done((f32[3,8,8,128]{3,2,1,0:T(8,128)S(1)}, f32[3,8,8,128]{3,2,1,0:T(8,128)}, u32[]{:S(2)}) %copy-start) | copy-done | bytes 98328
  1.5 29.5 %shard_map.41 = (f32[3,8,8,128]{3,2,1,0:T(8,128)S(1)}, f32[8,8,128]{2,1,0:T(8,128)S(1)}) custom-call(f32[3,8,8,128]{3,2,1,0:T(8,128)S(1)} %copy-done, s32[61,8,8,128]{3,2,1,0:T(8,128)} %intact_hbm.1), custom_call_target="tpu_custom_call" | custom-call | tf_op jit(solution)/shard_map/pallas_call | solution.py:490
  31.1 0.6 %copy.6 = f32[3,8,8,128]{3,2,1,0:T(8,128)} copy(f32[3,8,8,128]{3,2,1,0:T(8,128)S(1)} %get-tuple-element.4) | data formatting | bytes 196608
  31.7 0.6 %copy.7 = f32[8,8,128]{2,1,0:T(8,128)} copy(f32[8,8,128]{2,1,0:T(8,128)S(1)} %get-tuple-element.5) | data formatting | bytes 65536
Async XLA Ops:
  0.6 0.9 %copy-start = (f32[3,8,8,128]{3,2,1,0:T(8,128)S(1)}, f32[3,8,8,128]{3,2,1,0:T(8,128)}, u32[]{:S(2)}) copy-start(f32[3,8,8,128]{3,2,1,0:T(8,128)} %u_hbm.1) | copy-start | bytes 294916
